TPU v7x, 32 devices: a whole 2x2x4 slice. The times are simulated.
32 devices in a mesh: dp: 4 (over x, core), seq: 8 (over z, y).
Axes of the slice: x: 2, y: 2, z: 4, core: 2. Of those that a mesh axis runs over, the one named last changes fastest.
Arguments:
- q_raw: bfloat16 [4, 1024, 4096], P('dp', 'seq'), may hold values from -64 to 64
- k_raw: bfloat16 [4, 1024, 4096], P('dp', 'seq'), may hold values from -64 to 64
- values: bfloat16 [4, 1024, 4096], P('dp', 'seq'), may hold values from -6 to 6
- grad_out: bfloat16 [4, 1024, 4096], P('dp', 'seq'), may hold values from -6 to 6
- q_gain: float32 [4096], replicated, may hold values from 0.1 to 1.9
- k_gain: float32 [4096], replicated, may hold values from 0.1 to 1.9
- lengths: int32 [4, 6], P('dp'), may hold values from 1 to 341, 1024 in all within a row
- positions: int32 [4, 3, 1024], P('dp', None, 'seq'), may hold values from 0 to 63
Outputs:
- attended: bfloat16 [4, 1024, 4096], P('dp', 'seq')
- grad_q: bfloat16 [4, 1024, 4096], P('dp', 'seq')
- grad_k: bfloat16 [4, 1024, 4096], P('dp', 'seq')
- grad_v: bfloat16 [4, 1024, 4096], P('dp', 'seq')
- grad_q_gain: float32 [4096], replicated
- grad_k_gain: float32 [4096], replicated
Inputs may be any that keep to these rules, and one draw needn't show every extreme that they name: `lengths`: the clips of a bucket lie end to end and fill its 1024 tokens.
All inputs are finite; a program needn't handle non-finite values.
Results may differ from a plain program's by a relative error of at most 0.012.
The roundings to bfloat16 on the way count: a program that leaves them out, or rounds other values in their place, can miss the bound.
Values may be sent and summed in bfloat16 or wider, within the bound.
A program may use at most 128 MiB of HBM per device.

v0:
```python
import jax
import jax.numpy as jnp
from jax import lax
from jax.sharding import PartitionSpec as P

HEAD_DIM = 128
epsilon = 1e-06


def product(form, left, right):
    return jnp.einsum(form, left, right, preferred_element_type=jnp.float32)


def segment_ids(clip_lengths, tokens):
    boundary = jnp.cumsum(clip_lengths)
    places = jnp.arange(tokens, dtype=jnp.int32)
    return jnp.sum((boundary[None, :] <= places[:, None]).astype(jnp.int32), axis=1)


def rope_tables(position_rows, head_dim):
    half = head_dim // 2
    sixth = head_dim // 6
    first = half - 2 * sixth
    pairs = jnp.arange(half, dtype=jnp.int32)
    section = (pairs >= first).astype(jnp.int32) + (pairs >= first + sixth).astype(jnp.int32)
    begin = jnp.where(section == 0, 0, jnp.where(section == 1, first, first + sixth))
    number = jnp.where(section == 0, first, sixth)
    freqs = 10000.0 ** (-(pairs - begin).astype(jnp.float32) / number.astype(jnp.float32))
    picker = (section[None, :] == jnp.arange(3, dtype=jnp.int32)[:, None]).astype(
        jnp.float32
    ) * freqs[None, :]
    angle = lax.dot_general(
        position_rows.astype(jnp.float32),
        picker,
        (((0,), (0,)), ((), ())),
        precision=lax.Precision.HIGHEST,
    )
    cosine = jnp.cos(angle)
    sine = jnp.sin(angle)
    return (jnp.concatenate([cosine, cosine], axis=-1), jnp.concatenate([sine, sine], axis=-1))


def rotate_pairs(inputs, cosine, sine):
    half = inputs.shape[-1] // 2
    partner = jnp.concatenate([-inputs[..., half:], inputs[..., :half]], axis=-1)
    return inputs * cosine[:, None, :] + partner * sine[:, None, :]


def rotate_back(grads, cosine, sine):
    half = grads.shape[-1] // 2
    turned = grads * sine[:, None, :]
    return grads * cosine[:, None, :] + jnp.concatenate(
        [turned[..., half:], -turned[..., :half]], axis=-1
    )


def attention_forward(query, keys, value_rows, segment, block, window, reach):
    count = query.shape[0]
    scale = query.shape[2] ** (-0.5)

    def one_block(index_block):
        start = index_block * block
        key_start = jnp.clip(start - reach, 0, count - window)
        query_block = lax.dynamic_slice_in_dim(query, start, block, 0)
        key_window = lax.dynamic_slice_in_dim(keys, key_start, window, 0)
        value_window = lax.dynamic_slice_in_dim(value_rows, key_start, window, 0)
        query_clip = lax.dynamic_slice_in_dim(segment, start, block, 0)
        key_clip = lax.dynamic_slice_in_dim(segment, key_start, window, 0)
        scores = product("qhd,khd->hqk", query_block, key_window) * scale
        live = (query_clip[:, None] == key_clip[None, :])[None]
        scores = jnp.where(live, scores, -1e30)
        highest = jnp.max(scores, axis=-1, keepdims=True)
        expon = jnp.exp(scores - highest)
        totals = jnp.sum(expon, axis=-1, keepdims=True)
        weights = (expon / totals).astype(jnp.bfloat16)
        output = product("hqk,khd->qhd", weights, value_window)
        return (output, (highest + jnp.log(totals))[..., 0])

    outputs, logsum = lax.map(one_block, jnp.arange(count // block, dtype=jnp.int32))
    return (outputs.reshape(query.shape), logsum)


def attention_backward(
    query, keys, value_rows, context, cotangent, logsum, segment, block, window, reach
):
    count = query.shape[0]
    scale = query.shape[2] ** (-0.5)
    delta = jnp.sum(cotangent.astype(jnp.float32) * context.astype(jnp.float32), axis=-1)

    def one_block(carry, inputs):
        key_acc, value_acc = carry
        index_block, block_logsum = inputs
        start = index_block * block
        key_start = jnp.clip(start - reach, 0, count - window)
        query_block = lax.dynamic_slice_in_dim(query, start, block, 0)
        cot_block = lax.dynamic_slice_in_dim(cotangent, start, block, 0)
        delta_block = lax.dynamic_slice_in_dim(delta, start, block, 0)
        key_window = lax.dynamic_slice_in_dim(keys, key_start, window, 0)
        value_window = lax.dynamic_slice_in_dim(value_rows, key_start, window, 0)
        query_clip = lax.dynamic_slice_in_dim(segment, start, block, 0)
        key_clip = lax.dynamic_slice_in_dim(segment, key_start, window, 0)
        scores = product("qhd,khd->hqk", query_block, key_window) * scale
        live = (query_clip[:, None] == key_clip[None, :])[None]
        probs = jnp.where(live, jnp.exp(scores - block_logsum[:, :, None]), 0.0)
        prob_half = probs.astype(jnp.bfloat16)
        value_grad = product("hqk,qhd->khd", prob_half, cot_block)
        dprob = product("qhd,khd->hqk", cot_block, value_window)
        dscore = (probs * (dprob - jnp.transpose(delta_block)[:, :, None]) * scale).astype(
            jnp.bfloat16
        )
        query_grad = product("hqk,khd->qhd", dscore, key_window)
        key_grad = product("hqk,qhd->khd", dscore, query_block)
        key_acc = lax.dynamic_update_slice_in_dim(
            key_acc,
            lax.dynamic_slice_in_dim(key_acc, key_start, window, 0) + key_grad,
            key_start,
            0,
        )
        value_acc = lax.dynamic_update_slice_in_dim(
            value_acc,
            lax.dynamic_slice_in_dim(value_acc, key_start, window, 0) + value_grad,
            key_start,
            0,
        )
        return ((key_acc, value_acc), query_grad)

    zeros = jnp.zeros(query.shape, jnp.float32)
    indices = jnp.arange(count // block, dtype=jnp.int32)
    (key_acc, value_acc), query_grads = lax.scan(one_block, (zeros, zeros), (indices, logsum))
    return (query_grads.reshape(query.shape), key_acc, value_acc)


def on_device(q_raw, k_raw, values, grad_out, q_gain, k_gain, lengths, positions):
    members = lax.axis_size("seq")
    replicas = lax.axis_size("dp")
    tok_dev = q_raw.shape[1]
    feature = q_raw.shape[2]
    tokens = tok_dev * members
    share = feature // members
    local_heads = share // HEAD_DIM
    reach = tokens // 3
    block = min(512, tokens)
    window = min(tokens, block + 2 * reach)
    segment = segment_ids(lengths[0], tokens)
    cosine, sine = rope_tables(positions[0], HEAD_DIM)
    query_float = q_raw[0].astype(jnp.float32)
    key_float = k_raw[0].astype(jnp.float32)
    query_scale = lax.rsqrt(jnp.mean(query_float * query_float, axis=-1) + epsilon)
    key_scale = lax.rsqrt(jnp.mean(key_float * key_float, axis=-1) + epsilon)
    query_hat = query_float * query_scale[:, None]
    key_hat = key_float * key_scale[:, None]
    query_rot = rotate_pairs((query_hat * q_gain).reshape(tok_dev, -1, HEAD_DIM), cosine, sine)
    key_rot = rotate_pairs((key_hat * k_gain).reshape(tok_dev, -1, HEAD_DIM), cosine, sine)
    sent = (
        query_rot.astype(jnp.bfloat16).reshape(1, tok_dev, feature),
        key_rot.astype(jnp.bfloat16).reshape(1, tok_dev, feature),
        values,
    )
    got_query, got_key, got_value = (
        lax.all_to_all(sent[0], "seq", split_axis=2, concat_axis=1, tiled=True),
        lax.all_to_all(sent[1], "seq", split_axis=2, concat_axis=1, tiled=True),
        lax.all_to_all(sent[2], "seq", split_axis=2, concat_axis=1, tiled=True),
    )
    query_heads = got_query[0].reshape(tokens, local_heads, HEAD_DIM)
    key_heads = got_key[0].reshape(tokens, local_heads, HEAD_DIM)
    value_heads = got_value[0].reshape(tokens, local_heads, HEAD_DIM)
    context, logsum = attention_forward(
        query_heads, key_heads, value_heads, segment, block, window, reach
    )
    context_half = context.astype(jnp.bfloat16)
    attended = lax.all_to_all(
        context_half.reshape(1, tokens, share), "seq", split_axis=1, concat_axis=2, tiled=True
    )
    cotangent = lax.all_to_all(grad_out, "seq", split_axis=2, concat_axis=1, tiled=True)[0].reshape(
        tokens, local_heads, HEAD_DIM
    )
    query_grad, key_grad, value_grad = attention_backward(
        query_heads,
        key_heads,
        value_heads,
        context_half,
        cotangent,
        logsum,
        segment,
        block,
        window,
        reach,
    )
    query_half = query_grad.astype(jnp.bfloat16)
    key_half = key_grad.astype(jnp.bfloat16)
    value_half = value_grad.astype(jnp.bfloat16).reshape(1, tokens, share)
    sent_back = (
        query_half.reshape(1, tokens, share),
        key_half.reshape(1, tokens, share),
        value_half,
    )
    back_query, back_key, back_value = (
        lax.all_to_all(sent_back[0], "seq", split_axis=1, concat_axis=2, tiled=True),
        lax.all_to_all(sent_back[1], "seq", split_axis=1, concat_axis=2, tiled=True),
        lax.all_to_all(sent_back[2], "seq", split_axis=1, concat_axis=2, tiled=True),
    )
    query_back = rotate_back(
        back_query[0].astype(jnp.float32).reshape(tok_dev, -1, HEAD_DIM), cosine, sine
    ).reshape(tok_dev, feature)
    key_back = rotate_back(
        back_key[0].astype(jnp.float32).reshape(tok_dev, -1, HEAD_DIM), cosine, sine
    ).reshape(tok_dev, feature)
    query_part = jnp.sum(query_back * query_hat, axis=0)
    key_part = jnp.sum(key_back * key_hat, axis=0)
    query_lift = query_back * q_gain
    key_lift = key_back * k_gain
    query_input = query_scale[:, None] * (
        query_lift - query_hat * jnp.mean(query_lift * query_hat, axis=-1, keepdims=True)
    )
    key_input = key_scale[:, None] * (
        key_lift - key_hat * jnp.mean(key_lift * key_hat, axis=-1, keepdims=True)
    )
    gains = lax.psum(jnp.stack([query_part, key_part]), ("dp", "seq")) / replicas
    grad_query_input = query_input.astype(jnp.bfloat16)[None]
    grad_key_input = key_input.astype(jnp.bfloat16)[None]
    return (attended, grad_query_input, grad_key_input, back_value, gains[0], gains[1])


def solution(mesh):
    return jax.shard_map(
        on_device,
        mesh=mesh,
        in_specs=(
            P("dp", "seq", None),
            P("dp", "seq", None),
            P("dp", "seq", None),
            P("dp", "seq", None),
            P(),
            P(),
            P("dp", None),
            P("dp", None, "seq"),
        ),
        out_specs=(
            P("dp", "seq", None),
            P("dp", "seq", None),
            P("dp", "seq", None),
            P("dp", "seq", None),
            P(),
            P(),
        ),
        check_vma=False,
    )
```

profile of v0, /device:TPU:0, one launch (start us, length us, event | category | flops | bytes accessed | tf_op | source)
XLA Modules:
  0.0 501.7 jit_solution(1113454433465873790)
XLA Ops:
  12.2 16.7 %copy.213 = bf16[1,128,4096]{1,0,2:T(2,128)(2,1)S(1)} copy(bf16[1,128,4096]{1,2,0:T(8,128)(2,1)S(1)} %get-tuple-element.342) | data formatting | bytes 2097152 | tf_op jit(solution)/shard_map/convert_element_type | solution.py:155
  29.4 23.4 %reduce.10 = bf16[4096,128]{1,0:T(8,128)(2,1)} reduce(bf16[4096,1,128]{2,1,0:T(2,128)(2,1)S(1)} %bitcast.238, bf16[]{:T(256)} %broadcast.330), dimensions={1}, to_apply=%bitcast.188.reduce_sub_computation | reduce | bytes 2097154
  54.9 7.5 %all-to-all-start = ((bf16[8,2,32768]{2,1,0:T(2,128)(2,1)}), bf16[8,2,32768]{2,1,0:T(2,128)(2,1)}, u32[]{:S(2)}, u32[]{:S(2)}) async-start(bf16[8,2,32768]{2,1,0:T(2,128)(2,1)} %reshape.589), calls=%async_computation | async-start | bytes 2097152 | tf_op jit(solution)/shard_map/all_to_all | solution.py:160
  62.5 16.7 %copy.212 = bf16[1,128,4096]{1,0,2:T(2,128)(2,1)S(1)} copy(bf16[1,128,4096]{1,2,0:T(8,128)(2,1)S(1)} %get-tuple-element.341) | data formatting | bytes 2097152 | tf_op jit(solution)/shard_map/convert_element_type | solution.py:156
  79.2 22.4 %reduce.11 = bf16[4096,128]{1,0:T(8,128)(2,1)S(1)} reduce(bf16[4096,1,128]{2,1,0:T(2,128)(2,1)S(1)} %bitcast.241, bf16[]{:T(256)} %broadcast.330), dimensions={1}, to_apply=%bitcast.187.reduce_sub_computation | reduce | bytes 2097154
  102.7 6.0 %all-to-all-start.1 = ((bf16[8,2,32768]{2,1,0:T(2,128)(2,1)}), bf16[8,2,32768]{2,1,0:T(2,128)(2,1)S(1)}, u32[]{:S(2)}, u32[]{:S(2)}) async-start(bf16[8,2,32768]{2,1,0:T(2,128)(2,1)} %reshape.591), calls=%async_computation.1 | async-start | bytes 2097152 | tf_op jit(solution)/shard_map/all_to_all | solution.py:161
  113.8 23.4 %reduce.12 = bf16[4096,128]{1,0:T(8,128)(2,1)} reduce(bf16[4096,1,128]{2,1,0:T(2,128)(2,1)S(1)} %bitcast.245, bf16[]{:T(256)} %broadcast.330), dimensions={1}, to_apply=%bitcast.164.reduce_sub_computation | reduce | bytes 2097154
  139.3 6.3 %all-to-all-start.2 = ((bf16[8,2,32768]{2,1,0:T(2,128)(2,1)}), bf16[8,2,32768]{2,1,0:T(2,128)(2,1)}, u32[]{:S(2)}, u32[]{:S(2)}) async-start(bf16[8,2,32768]{2,1,0:T(2,128)(2,1)} %reshape.593), calls=%async_computation.2 | async-start | bytes 2097152 | tf_op jit(solution)/shard_map/all_to_all | solution.py:162
  145.8 5.5 %copy.167 = bf16[1,128,4096]{1,0,2:T(2,128)(2,1)} copy(bf16[1,128,4096]{2,1,0:T(8,128)(2,1)} %param.15) | data formatting | bytes 2097152 | tf_op args[3]
  151.3 24.4 %reduce.14 = bf16[4096,128]{1,0:T(8,128)(2,1)} reduce(bf16[4096,1,128]{2,1,0:T(2,128)(2,1)} %bitcast.246, bf16[]{:T(256)} %broadcast.330), dimensions={1}, to_apply=%bitcast.168.reduce_sub_computation | reduce | bytes 2097154
  177.9 5.8 %reshape.590 = bf16[4096,1,128]{2,1,0:T(2,128)(2,1)} reshape(bf16[8,2,32768]{2,1,0:T(2,128)(2,1)} %all-to-all-done) | data formatting | bytes 2097152
  200.4 6.5 %all-to-all-start.4 = ((bf16[8,2,32768]{2,1,0:T(2,128)(2,1)}), bf16[8,2,32768]{2,1,0:T(2,128)(2,1)}, u32[]{:S(2)}, u32[]{:S(2)}) async-start(bf16[8,2,32768]{2,1,0:T(2,128)(2,1)} %reshape.597), calls=%async_computation.4 | async-start | bytes 2097152 | tf_op jit(solution)/shard_map/all_to_all | solution.py:174
  206.8 5.8 %reshape.594 = bf16[4096,1,128]{2,1,0:T(2,128)(2,1)} reshape(bf16[8,2,32768]{2,1,0:T(2,128)(2,1)} %all-to-all-done.2) | data formatting | bytes 2097152
  221.7 21.2 %while.27 = (s32[]{:T(128)}, bf16[2,512,4,128]{3,1,2,0:T(8,128)(2,1)}, f32[2,4,512]{2,1,0:T(4,128)S(1)}, s32[2]{0:T(128)S(1)}, s32[1024]{0:T(1024)S(1)}, /*index...) while((s32[]{:T(128)}, ...), condition=%wide.region_7.8_spmd, body=%wide.region_4.7_spmd.sunk | while | flops 1099429888 | bytes 35203796 | solution.py:79
  250.7 5.8 %reshape.598 = bf16[4096,1,128]{2,1,0:T(2,128)(2,1)} reshape(bf16[8,2,32768]{2,1,0:T(2,128)(2,1)} %all-to-all-done.4) | data formatting | bytes 2097152
  265.4 47.3 %while.28 = (s32[]{:T(128)}, f32[1024,4,128]{0,2,1:T(8,128)S(1)}, f32[1024,4,128]{0,2,1:T(8,128)}, bf16[2,512,4,128]{3,1,2,0:T(8,128)(2,1)}, s32[2]{0:T(128)S(1)...) while((s32[]{:T(128)}, f32[1024,4,128]{0,2,1:T(8,128)S(1)}, ...), condition=%wide.region_10.11_spmd.clone, body=%wide.region_9.10_spmd.clone.sunk | while | flops 2710044672 | bytes 154733552 | solution.py:129
  318.1 8.0 %reduce.16 = bf16[1024,512]{1,0:T(8,128)(2,1)S(1)} reduce(bf16[1024,1,512]{2,1,0:T(2,128)(2,1)} %bitcast.242, bf16[]{:T(256)} %broadcast.330), dimensions={1}, to_apply=%bitcast.170.reduce_sub_computation | reduce | bytes 2097154
  327.7 6.3 %all-to-all-start.5 = ((bf16[8,2,32768]{2,1,0:T(2,128)(2,1)}), bf16[8,2,32768]{2,1,0:T(2,128)(2,1)}, u32[]{:S(2)}, u32[]{:S(2)}) async-start(bf16[8,2,32768]{2,1,0:T(2,128)(2,1)} %reshape.599), calls=%async_computation.5 | async-start | bytes 2097152 | tf_op jit(solution)/shard_map/all_to_all | solution.py:198
  336.1 7.0 %reduce.15 = bf16[1024,512]{1,0:T(8,128)(2,1)S(1)} reduce(bf16[1024,1,512]{2,1,0:T(2,128)(2,1)S(1)} %bitcast.243, bf16[]{:T(256)} %broadcast.330), dimensions={1}, to_apply=%bitcast.172.reduce_sub_computation | reduce | bytes 2097154
  344.7 13.1 %all-to-all-done.5 = bf16[8,2,32768]{2,1,0:T(2,128)(2,1)} async-done(((bf16[8,2,32768]{2,1,0:T(2,128)(2,1)}), bf16[8,2,32768]{2,1,0:T(2,128)(2,1)}, u32[]{:S(2)}, u32[]{:S(2)}) %all-to-all-start.5) | async-done | bytes 1048608 | tf_op jit(solution)/shard_map/all_to_all | solution.py:198
  374.3 8.1 %reduce.17 = bf16[1024,512]{1,0:T(8,128)(2,1)} reduce(bf16[1024,1,512]{2,1,0:T(2,128)(2,1)S(1)} %bitcast.244, bf16[]{:T(256)} %broadcast.330), dimensions={1}, to_apply=%bitcast.174.reduce_sub_computation | reduce | bytes 2097154
  385.7 7.0 %reduce.13 = bf16[1024,512]{1,0:T(8,128)(2,1)S(1)} reduce(bf16[1024,1,512]{2,1,0:T(2,128)(2,1)S(1)} %bitcast.240, bf16[]{:T(256)} %broadcast.330), dimensions={1}, to_apply=%bitcast.166.reduce_sub_computation | reduce | bytes 2097154
  403.6 6.0 %all-to-all-start.7 = ((bf16[8,2,32768]{2,1,0:T(2,128)(2,1)}), bf16[8,2,32768]{2,1,0:T(2,128)(2,1)}, u32[]{:S(2)}, u32[]{:S(2)}) async-start(bf16[8,2,32768]{2,1,0:T(2,128)(2,1)} %reshape.603), calls=%async_computation.7 | async-start | bytes 2097152 | tf_op jit(solution)/shard_map/all_to_all | solution.py:200
  453.4 40.8 %psum.7 = f32[2,4096]{1,0:T(2,128)S(1)} all-reduce(f32[2,4096]{1,0:T(2,128)S(1)} %pad_maximum_fusion.4), channel_id=1, replica_groups=mesh['dp'=4,'seq'=8] {'dp','seq'}, use_global_device_ids=true, to_apply=%region_15.16 | all-reduce | flops 8192 | bytes 65536 | tf_op jit(solution)/shard_map/psum | solution.py:218
  (236 shorter events, 224.5 us)
Async XLA Ops:
  2.3 8.3 %copy-start.3 = (bf16[1,128,4096]{1,2,0:T(8,128)(2,1)}, bf16[1,128,4096]{1,2,0:T(8,128)(2,1)S(1)}, u32[]{:S(2)}) copy-start(bf16[1,128,4096]{1,2,0:T(8,128)(2,1)S(1)} %copy.156) | copy-start | bytes 3145732
  5.0 5.6 %copy-start.5 = (bf16[1,128,4096]{1,2,0:T(8,128)(2,1)}, bf16[1,128,4096]{1,2,0:T(8,128)(2,1)S(1)}, u32[]{:S(2)}) copy-start(bf16[1,128,4096]{1,2,0:T(8,128)(2,1)S(1)} %copy.153) | copy-start | bytes 3145732
  5.8 4.8 copy-start.31
  5.8 4.8 copy-start.33
  54.9 47.8 %all-to-all-start = ((bf16[8,2,32768]{2,1,0:T(2,128)(2,1)}), bf16[8,2,32768]{2,1,0:T(2,128)(2,1)}, u32[]{:S(2)}, u32[]{:S(2)}) async-start(bf16[8,2,32768]{2,1,0:T(2,128)(2,1)} %reshape.589), calls=%async_computation | async-start | bytes 2097152 | tf_op jit(solution)/shard_map/all_to_all | solution.py:160
  102.7 36.5 %all-to-all-start.1 = ((bf16[8,2,32768]{2,1,0:T(2,128)(2,1)}), bf16[8,2,32768]{2,1,0:T(2,128)(2,1)S(1)}, u32[]{:S(2)}, u32[]{:S(2)}) async-start(bf16[8,2,32768]{2,1,0:T(2,128)(2,1)} %reshape.591), calls=%async_computation.1 | async-start | bytes 2097152 | tf_op jit(solution)/shard_map/all_to_all | solution.py:161
  137.1 8.4 %copy-start.36 = (s32[1,6]{1,0:T(1,128)S(1)}, s32[1,6]{1,0:T(1,128)}, u32[]{:S(2)}) copy-start(s32[1,6]{1,0:T(1,128)} %param.18) | copy-start | bytes 76
  139.3 61.1 %all-to-all-start.2 = ((bf16[8,2,32768]{2,1,0:T(2,128)(2,1)}), bf16[8,2,32768]{2,1,0:T(2,128)(2,1)}, u32[]{:S(2)}, u32[]{:S(2)}) async-start(bf16[8,2,32768]{2,1,0:T(2,128)(2,1)} %reshape.593), calls=%async_computation.2 | async-start | bytes 2097152 | tf_op jit(solution)/shard_map/all_to_all | solution.py:162
  200.4 50.3 %all-to-all-start.4 = ((bf16[8,2,32768]{2,1,0:T(2,128)(2,1)}), bf16[8,2,32768]{2,1,0:T(2,128)(2,1)}, u32[]{:S(2)}, u32[]{:S(2)}) async-start(bf16[8,2,32768]{2,1,0:T(2,128)(2,1)} %reshape.597), calls=%async_computation.4 | async-start | bytes 2097152 | tf_op jit(solution)/shard_map/all_to_all | solution.py:174
  266.8 5.9 %copy-start.15 = (bf16[1024,4,128]{0,2,1:T(8,128)(2,1)S(1)}, bf16[1024,4,128]{0,2,1:T(8,128)(2,1)}, u32[]{:S(2)}) copy-start(bf16[1024,4,128]{0,2,1:T(8,128)(2,1)} %get-tuple-element.556) | copy-start | bytes 3145732 | tf_op jit(solution)/shard_map/while
  266.9 5.9 %copy-start.24 = (bf16[1024,4,128]{2,0,1:T(8,128)(2,1)S(1)}, bf16[1024,4,128]{2,0,1:T(8,128)(2,1)}, u32[]{:S(2)}) copy-start(bf16[1024,4,128]{2,0,1:T(8,128)(2,1)} %get-tuple-element.557) | copy-start | bytes 3145732 | tf_op jit(solution)/shard_map/while
  277.8 6.2 %copy-start.2 = (f32[4,512,1024]{2,1,0:T(8,128)S(1)}, f32[4,512,1024]{2,1,0:T(8,128)}, u32[]{:S(2)}) copy-start(f32[4,512,1024]{2,1,0:T(8,128)} %copy-done.1) | copy-start | bytes 25165828 | tf_op jit(solution)/shard_map/while
  289.8 5.9 %copy-start.15 = (bf16[1024,4,128]{0,2,1:T(8,128)(2,1)S(1)}, bf16[1024,4,128]{0,2,1:T(8,128)(2,1)}, u32[]{:S(2)}) copy-start(bf16[1024,4,128]{0,2,1:T(8,128)(2,1)} %get-tuple-element.556) | copy-start | bytes 3145732 | tf_op jit(solution)/shard_map/while
  289.8 5.9 %copy-start.24 = (bf16[1024,4,128]{2,0,1:T(8,128)(2,1)S(1)}, bf16[1024,4,128]{2,0,1:T(8,128)(2,1)}, u32[]{:S(2)}) copy-start(bf16[1024,4,128]{2,0,1:T(8,128)(2,1)} %get-tuple-element.557) | copy-start | bytes 3145732 | tf_op jit(solution)/shard_map/while
  300.8 6.2 %copy-start.2 = (f32[4,512,1024]{2,1,0:T(8,128)S(1)}, f32[4,512,1024]{2,1,0:T(8,128)}, u32[]{:S(2)}) copy-start(f32[4,512,1024]{2,1,0:T(8,128)} %copy-done.1) | copy-start | bytes 25165828 | tf_op jit(solution)/shard_map/while
  327.7 30.1 %all-to-all-start.5 = ((bf16[8,2,32768]{2,1,0:T(2,128)(2,1)}), bf16[8,2,32768]{2,1,0:T(2,128)(2,1)}, u32[]{:S(2)}, u32[]{:S(2)}) async-start(bf16[8,2,32768]{2,1,0:T(2,128)(2,1)} %reshape.599), calls=%async_computation.5 | async-start | bytes 2097152 | tf_op jit(solution)/shard_map/all_to_all | solution.py:198
  343.1 19.4 %copy-start.30 = (f32[4096]{0:T(1024)S(1)}, f32[4096]{0:T(1024)}, u32[]{:S(2)}) copy-start(f32[4096]{0:T(1024)} %param.16) | copy-start | bytes 49156
  343.1 19.4 %copy-start.28 = (f32[4096]{0:T(1024)S(1)}, f32[4096]{0:T(1024)}, u32[]{:S(2)}) copy-start(f32[4096]{0:T(1024)} %param.17) | copy-start | bytes 49156
  343.1 19.5 %copy-start.21 = (f32[128,128]{0,1:T(8,128)S(1)}, f32[128,128]{0,1:T(8,128)}, u32[]{:S(2)}) copy-start(f32[128,128]{0,1:T(8,128)} %copy-done.20) | copy-start | bytes 196612
  357.8 45.8 %all-to-all-start.6 = ((bf16[8,2,32768]{2,1,0:T(2,128)(2,1)}), bf16[8,2,32768]{2,1,0:T(2,128)(2,1)}, u32[]{:S(2)}, u32[]{:S(2)}) async-start(bf16[8,2,32768]{2,1,0:T(2,128)(2,1)} %reshape.601), calls=%async_computation.6 | async-start | bytes 2097152 | tf_op jit(solution)/shard_map/all_to_all | solution.py:199
  374.3 10.7 %copy-start.17 = (bf16[2,512,4,128]{3,2,1,0:T(4,128)(2,1)S(1)}, bf16[2,512,4,128]{3,2,1,0:T(4,128)(2,1)}, u32[]{:S(2)}) copy-start(bf16[2,512,4,128]{3,2,1,0:T(4,128)(2,1)} %copy.164) | copy-start | bytes 3145732
  403.6 30.2 %all-to-all-start.7 = ((bf16[8,2,32768]{2,1,0:T(2,128)(2,1)}), bf16[8,2,32768]{2,1,0:T(2,128)(2,1)}, u32[]{:S(2)}, u32[]{:S(2)}) async-start(bf16[8,2,32768]{2,1,0:T(2,128)(2,1)} %reshape.603), calls=%async_computation.7 | async-start | bytes 2097152 | tf_op jit(solution)/shard_map/all_to_all | solution.py:200
  431.4 6.9 %copy-start.4 = (bf16[1,128,4096]{1,2,0:T(8,128)(2,1)S(1)}, bf16[1,128,4096]{1,2,0:T(8,128)(2,1)}, u32[]{:S(2)}) copy-start(bf16[1,128,4096]{1,2,0:T(8,128)(2,1)} %copy-done.3) | copy-start | bytes 3145732
  433.8 61.0 %all-to-all-start.3 = ((bf16[8,2,32768]{2,1,0:T(2,128)(2,1)}), bf16[8,2,32768]{2,1,0:T(2,128)(2,1)}, u32[]{:S(2)}, u32[]{:S(2)}) async-start(bf16[8,2,32768]{2,1,0:T(2,128)(2,1)} %reshape.595), calls=%async_computation.3 | async-start | bytes 2097152 | tf_op jit(solution)/shard_map/all_to_all | solution.py:171
  (30 other events, 76.9 us)
where the time goes:
time: 511 us; the launch traced here: 502 us
  local copies, waits for them, and re-layouts  186 us (36%)
  other arithmetic  159 us (31%)
  matrix products  48.8 us (10%)
  starting transfers between devices  47.7 us (9%)
  blocking collectives  40.8 us (8%)
  waiting for transfers between devices  15.5 us (3%)
    unnamed x10, other arithmetic  124 us
    unnamed x89, local copies, waits for them, and re-layouts  85 us
    dot_general x14, matrix products, product(): return jnp.einsum(form, left, right, preferred_element_type=jnp.float32)  48.4 us
    psum x1, blocking collectives, on_device(): lax.psum(jnp.stack([query_part, key_part]), ('dp', 'seq')) / replicas  40.8 us
    convert_element_type x1, local copies, waits for them, and re-layouts, on_device(): query_rot.astype(jnp.bfloat16).reshape(1, tok_dev, feature)  16.7 us
    convert_element_type x1, local copies, waits for them, and re-layouts, on_device(): key_rot.astype(jnp.bfloat16).reshape(1, tok_dev, feature)  16.7 us
    all_to_all x1, waiting for transfers between devices, on_device(): lax.all_to_all(sent_back[0], 'seq', split_axis=1, concat_axis=2, tiled=True)  13.1 us
  transfers between devices with their start and end apart: 8, of which 2 were waited for; matrix products, arithmetic and copies ran while one was open for 51% of the time, Pallas kernels for 0%

commit v1 on v0

--- a/solution.py
+++ b/solution.py
@@ -5,6 +5,11 @@
 
 HEAD_DIM = 128
 epsilon = 1e-06
+
+
+def axis_by_axis(value, leading, second):
+    partial = lax.psum(value, leading)
+    return lax.psum(partial, second)
 
 
 def product(form, left, right):
@@ -215,7 +220,7 @@
     key_input = key_scale[:, None] * (
         key_lift - key_hat * jnp.mean(key_lift * key_hat, axis=-1, keepdims=True)
     )
-    gains = lax.psum(jnp.stack([query_part, key_part]), ("dp", "seq")) / replicas
+    gains = axis_by_axis(jnp.stack([query_part, key_part]), "seq", "dp") / replicas
     grad_query_input = query_input.astype(jnp.bfloat16)[None]
     grad_key_input = key_input.astype(jnp.bfloat16)[None]
     return (attended, grad_query_input, grad_key_input, back_value, gains[0], gains[1])

time: 511 us -> 529 us (1.035)
  blocking collectives: 40.8 us -> 58.5 us
    psum x1 -> x2, blocking collectives: 40.8 us -> 58.5 us  [the longest x1 48.3 us: axis_by_axis(): partial = lax.psum(value, leading)]
  transfers between devices with their start and end apart: 8 -> 8, of which waited for: 2 -> 2; matrix products, arithmetic and copies ran while one was open for 51% -> 49% of each run, Pallas kernels for 0% -> 0%
where the time goes in v1:
time: 529 us; the launch traced here: 519 us
  local copies, waits for them, and re-layouts  186 us (35%)
  other arithmetic  158 us (30%)
  blocking collectives  58.5 us (11%)
  matrix products  48.9 us (9%)
  starting transfers between devices  47.5 us (9%)
  waiting for transfers between devices  15.5 us (3%)
    unnamed x10, other arithmetic  124 us
    unnamed x89, local copies, waits for them, and re-layouts  85.1 us
    dot_general x14, matrix products, product(): return jnp.einsum(form, left, right, preferred_element_type=jnp.float32)  48.5 us
    psum x1, blocking collectives, axis_by_axis(): partial = lax.psum(value, leading)  48.3 us
    convert_element_type x1, local copies, waits for them, and re-layouts, on_device(): query_rot.astype(jnp.bfloat16).reshape(1, tok_dev, feature)  16.7 us
    convert_element_type x1, local copies, waits for them, and re-layouts, on_device(): key_rot.astype(jnp.bfloat16).reshape(1, tok_dev, feature)  16.7 us
    all_to_all x1, waiting for transfers between devices, on_device(): lax.all_to_all(sent_back[0], 'seq', split_axis=1, concat_axis=2, tiled=True)  13.1 us
  transfers between devices with their start and end apart: 8, of which 2 were waited for; matrix products, arithmetic and copies ran while one was open for 49% of the time, Pallas kernels for 0%

profile of v1, /device:TPU:0, one launch (start us, length us, event | category | flops | bytes accessed | tf_op | source)
XLA Modules:
  0.0 519.3 jit_solution(11859626062586112865)
XLA Ops:
  12.2 16.7 %copy.213 = bf16[1,128,4096]{1,0,2:T(2,128)(2,1)S(1)} copy(bf16[1,128,4096]{1,2,0:T(8,128)(2,1)S(1)} %get-tuple-element.342) | data formatting | bytes 2097152 | tf_op jit(solution)/shard_map/convert_element_type | solution.py:160
  29.5 23.4 %reduce.10 = bf16[4096,128]{1,0:T(8,128)(2,1)} reduce(bf16[4096,1,128]{2,1,0:T(2,128)(2,1)S(1)} %bitcast.238, bf16[]{:T(256)} %broadcast.330), dimensions={1}, to_apply=%bitcast.188.reduce_sub_computation | reduce | bytes 2097154
  54.9 7.5 %all-to-all-start = ((bf16[8,2,32768]{2,1,0:T(2,128)(2,1)}), bf16[8,2,32768]{2,1,0:T(2,128)(2,1)}, u32[]{:S(2)}, u32[]{:S(2)}) async-start(bf16[8,2,32768]{2,1,0:T(2,128)(2,1)} %reshape.589), calls=%async_computation | async-start | bytes 2097152 | tf_op jit(solution)/shard_map/all_to_all | solution.py:165
  62.5 16.7 %copy.212 = bf16[1,128,4096]{1,0,2:T(2,128)(2,1)S(1)} copy(bf16[1,128,4096]{1,2,0:T(8,128)(2,1)S(1)} %get-tuple-element.341) | data formatting | bytes 2097152 | tf_op jit(solution)/shard_map/convert_element_type | solution.py:161
  79.2 22.4 %reduce.11 = bf16[4096,128]{1,0:T(8,128)(2,1)S(1)} reduce(bf16[4096,1,128]{2,1,0:T(2,128)(2,1)S(1)} %bitcast.241, bf16[]{:T(256)} %broadcast.330), dimensions={1}, to_apply=%bitcast.187.reduce_sub_computation | reduce | bytes 2097154
  102.7 6.0 %all-to-all-start.1 = ((bf16[8,2,32768]{2,1,0:T(2,128)(2,1)}), bf16[8,2,32768]{2,1,0:T(2,128)(2,1)S(1)}, u32[]{:S(2)}, u32[]{:S(2)}) async-start(bf16[8,2,32768]{2,1,0:T(2,128)(2,1)} %reshape.591), calls=%async_computation.1 | async-start | bytes 2097152 | tf_op jit(solution)/shard_map/all_to_all | solution.py:166
  113.8 23.4 %reduce.12 = bf16[4096,128]{1,0:T(8,128)(2,1)} reduce(bf16[4096,1,128]{2,1,0:T(2,128)(2,1)S(1)} %bitcast.245, bf16[]{:T(256)} %broadcast.330), dimensions={1}, to_apply=%bitcast.164.reduce_sub_computation | reduce | bytes 2097154
  139.3 6.3 %all-to-all-start.2 = ((bf16[8,2,32768]{2,1,0:T(2,128)(2,1)}), bf16[8,2,32768]{2,1,0:T(2,128)(2,1)}, u32[]{:S(2)}, u32[]{:S(2)}) async-start(bf16[8,2,32768]{2,1,0:T(2,128)(2,1)} %reshape.593), calls=%async_computation.2 | async-start | bytes 2097152 | tf_op jit(solution)/shard_map/all_to_all | solution.py:167
  151.3 24.4 %reduce.14 = bf16[4096,128]{1,0:T(8,128)(2,1)} reduce(bf16[4096,1,128]{2,1,0:T(2,128)(2,1)} %bitcast.246, bf16[]{:T(256)} %broadcast.330), dimensions={1}, to_apply=%bitcast.168.reduce_sub_computation | reduce | bytes 2097154
  177.9 5.8 %reshape.590 = bf16[4096,1,128]{2,1,0:T(2,128)(2,1)} reshape(bf16[8,2,32768]{2,1,0:T(2,128)(2,1)} %all-to-all-done) | data formatting | bytes 2097152
  200.4 6.5 %all-to-all-start.4 = ((bf16[8,2,32768]{2,1,0:T(2,128)(2,1)}), bf16[8,2,32768]{2,1,0:T(2,128)(2,1)}, u32[]{:S(2)}, u32[]{:S(2)}) async-start(bf16[8,2,32768]{2,1,0:T(2,128)(2,1)} %reshape.597), calls=%async_computation.4 | async-start | bytes 2097152 | tf_op jit(solution)/shard_map/all_to_all | solution.py:179
  206.9 5.8 %reshape.594 = bf16[4096,1,128]{2,1,0:T(2,128)(2,1)} reshape(bf16[8,2,32768]{2,1,0:T(2,128)(2,1)} %all-to-all-done.2) | data formatting | bytes 2097152
  221.7 21.2 %while.27 = (s32[]{:T(128)}, bf16[2,512,4,128]{3,1,2,0:T(8,128)(2,1)}, f32[2,4,512]{2,1,0:T(4,128)S(1)}, s32[2]{0:T(128)S(1)}, s32[1024]{0:T(1024)S(1)}, /*index...) while((s32[]{:T(128)}, ...), condition=%wide.region_7.8_spmd, body=%wide.region_4.7_spmd.sunk | while | flops 1099429888 | bytes 35203796 | solution.py:84
  250.7 5.8 %reshape.598 = bf16[4096,1,128]{2,1,0:T(2,128)(2,1)} reshape(bf16[8,2,32768]{2,1,0:T(2,128)(2,1)} %all-to-all-done.4) | data formatting | bytes 2097152
  265.5 47.4 %while.28 = (s32[]{:T(128)}, f32[1024,4,128]{0,2,1:T(8,128)S(1)}, f32[1024,4,128]{0,2,1:T(8,128)}, bf16[2,512,4,128]{3,1,2,0:T(8,128)(2,1)}, s32[2]{0:T(128)S(1)...) while((s32[]{:T(128)}, f32[1024,4,128]{0,2,1:T(8,128)S(1)}, ...), condition=%wide.region_10.11_spmd.clone, body=%wide.region_9.10_spmd.clone.sunk | while | flops 2710044672 | bytes 154733552 | solution.py:134
  318.2 8.0 %reduce.16 = bf16[1024,512]{1,0:T(8,128)(2,1)S(1)} reduce(bf16[1024,1,512]{2,1,0:T(2,128)(2,1)} %bitcast.242, bf16[]{:T(256)} %broadcast.330), dimensions={1}, to_apply=%bitcast.170.reduce_sub_computation | reduce | bytes 2097154
  327.9 6.3 %all-to-all-start.5 = ((bf16[8,2,32768]{2,1,0:T(2,128)(2,1)}), bf16[8,2,32768]{2,1,0:T(2,128)(2,1)}, u32[]{:S(2)}, u32[]{:S(2)}) async-start(bf16[8,2,32768]{2,1,0:T(2,128)(2,1)} %reshape.599), calls=%async_computation.5 | async-start | bytes 2097152 | tf_op jit(solution)/shard_map/all_to_all | solution.py:203
  336.2 7.0 %reduce.15 = bf16[1024,512]{1,0:T(8,128)(2,1)S(1)} reduce(bf16[1024,1,512]{2,1,0:T(2,128)(2,1)S(1)} %bitcast.243, bf16[]{:T(256)} %broadcast.330), dimensions={1}, to_apply=%bitcast.172.reduce_sub_computation | reduce | bytes 2097154
  344.8 13.1 %all-to-all-done.5 = bf16[8,2,32768]{2,1,0:T(2,128)(2,1)} async-done(((bf16[8,2,32768]{2,1,0:T(2,128)(2,1)}), bf16[8,2,32768]{2,1,0:T(2,128)(2,1)}, u32[]{:S(2)}, u32[]{:S(2)}) %all-to-all-start.5) | async-done | bytes 1048608 | tf_op jit(solution)/shard_map/all_to_all | solution.py:203
  374.5 8.1 %reduce.17 = bf16[1024,512]{1,0:T(8,128)(2,1)} reduce(bf16[1024,1,512]{2,1,0:T(2,128)(2,1)S(1)} %bitcast.244, bf16[]{:T(256)} %broadcast.330), dimensions={1}, to_apply=%bitcast.174.reduce_sub_computation | reduce | bytes 2097154
  385.9 7.0 %reduce.13 = bf16[1024,512]{1,0:T(8,128)(2,1)S(1)} reduce(bf16[1024,1,512]{2,1,0:T(2,128)(2,1)S(1)} %bitcast.240, bf16[]{:T(256)} %broadcast.330), dimensions={1}, to_apply=%bitcast.166.reduce_sub_computation | reduce | bytes 2097154
  403.7 6.0 %all-to-all-start.7 = ((bf16[8,2,32768]{2,1,0:T(2,128)(2,1)}), bf16[8,2,32768]{2,1,0:T(2,128)(2,1)}, u32[]{:S(2)}, u32[]{:S(2)}) async-start(bf16[8,2,32768]{2,1,0:T(2,128)(2,1)} %reshape.603), calls=%async_computation.7 | async-start | bytes 2097152 | tf_op jit(solution)/shard_map/all_to_all | solution.py:205
  438.3 48.3 %psum.14 = f32[2,4096]{1,0:T(2,128)S(1)} all-reduce(f32[2,4096]{1,0:T(2,128)S(1)} %pad_maximum_fusion.4), channel_id=1, replica_groups=mesh['dp'=4,'seq'=8] {'seq'}, use_global_device_ids=true, to_apply=%region_15.16 | all-reduce | flops 8192 | bytes 65536 | tf_op jit(solution)/shard_map/psum | solution.py:11
  501.6 10.3 %psum.15 = f32[2,4096]{1,0:T(2,128)S(1)} all-reduce(f32[2,4096]{1,0:T(2,128)S(1)} %psum.14), channel_id=1, replica_groups=mesh['dp'=4,'seq'=8] {'dp'}, use_global_device_ids=true, to_apply=%region_16.17 | all-reduce | flops 8192 | bytes 65536 | tf_op jit(solution)/shard_map/psum | solution.py:12
  (237 shorter events, 229.9 us)
Async XLA Ops:
  2.3 8.3 %copy-start.3 = (bf16[1,128,4096]{1,2,0:T(8,128)(2,1)}, bf16[1,128,4096]{1,2,0:T(8,128)(2,1)S(1)}, u32[]{:S(2)}) copy-start(bf16[1,128,4096]{1,2,0:T(8,128)(2,1)S(1)} %copy.156) | copy-start | bytes 3145732
  5.0 5.6 %copy-start.5 = (bf16[1,128,4096]{1,2,0:T(8,128)(2,1)}, bf16[1,128,4096]{1,2,0:T(8,128)(2,1)S(1)}, u32[]{:S(2)}) copy-start(bf16[1,128,4096]{1,2,0:T(8,128)(2,1)S(1)} %copy.153) | copy-start | bytes 3145732
  5.8 4.8 copy-start.31
  5.8 4.8 copy-start.33
  54.9 47.8 %all-to-all-start = ((bf16[8,2,32768]{2,1,0:T(2,128)(2,1)}), bf16[8,2,32768]{2,1,0:T(2,128)(2,1)}, u32[]{:S(2)}, u32[]{:S(2)}) async-start(bf16[8,2,32768]{2,1,0:T(2,128)(2,1)} %reshape.589), calls=%async_computation | async-start | bytes 2097152 | tf_op jit(solution)/shard_map/all_to_all | solution.py:165
  102.7 36.5 %all-to-all-start.1 = ((bf16[8,2,32768]{2,1,0:T(2,128)(2,1)}), bf16[8,2,32768]{2,1,0:T(2,128)(2,1)S(1)}, u32[]{:S(2)}, u32[]{:S(2)}) async-start(bf16[8,2,32768]{2,1,0:T(2,128)(2,1)} %reshape.591), calls=%async_computation.1 | async-start | bytes 2097152 | tf_op jit(solution)/shard_map/all_to_all | solution.py:166
  137.1 8.4 %copy-start.36 = (s32[1,6]{1,0:T(1,128)S(1)}, s32[1,6]{1,0:T(1,128)}, u32[]{:S(2)}) copy-start(s32[1,6]{1,0:T(1,128)} %param.18) | copy-start | bytes 76
  139.3 61.1 %all-to-all-start.2 = ((bf16[8,2,32768]{2,1,0:T(2,128)(2,1)}), bf16[8,2,32768]{2,1,0:T(2,128)(2,1)}, u32[]{:S(2)}, u32[]{:S(2)}) async-start(bf16[8,2,32768]{2,1,0:T(2,128)(2,1)} %reshape.593), calls=%async_computation.2 | async-start | bytes 2097152 | tf_op jit(solution)/shard_map/all_to_all | solution.py:167
  200.4 50.4 %all-to-all-start.4 = ((bf16[8,2,32768]{2,1,0:T(2,128)(2,1)}), bf16[8,2,32768]{2,1,0:T(2,128)(2,1)}, u32[]{:S(2)}, u32[]{:S(2)}) async-start(bf16[8,2,32768]{2,1,0:T(2,128)(2,1)} %reshape.597), calls=%async_computation.4 | async-start | bytes 2097152 | tf_op jit(solution)/shard_map/all_to_all | solution.py:179
  266.9 5.9 %copy-start.15 = (bf16[1024,4,128]{0,2,1:T(8,128)(2,1)S(1)}, bf16[1024,4,128]{0,2,1:T(8,128)(2,1)}, u32[]{:S(2)}) copy-start(bf16[1024,4,128]{0,2,1:T(8,128)(2,1)} %get-tuple-element.556) | copy-start | bytes 3145732 | tf_op jit(solution)/shard_map/while
  266.9 5.9 %copy-start.24 = (bf16[1024,4,128]{2,0,1:T(8,128)(2,1)S(1)}, bf16[1024,4,128]{2,0,1:T(8,128)(2,1)}, u32[]{:S(2)}) copy-start(bf16[1024,4,128]{2,0,1:T(8,128)(2,1)} %get-tuple-element.557) | copy-start | bytes 3145732 | tf_op jit(solution)/shard_map/while
  277.9 6.2 %copy-start.2 = (f32[4,512,1024]{2,1,0:T(8,128)S(1)}, f32[4,512,1024]{2,1,0:T(8,128)}, u32[]{:S(2)}) copy-start(f32[4,512,1024]{2,1,0:T(8,128)} %copy-done.1) | copy-start | bytes 25165828 | tf_op jit(solution)/shard_map/while
  289.9 5.9 %copy-start.15 = (bf16[1024,4,128]{0,2,1:T(8,128)(2,1)S(1)}, bf16[1024,4,128]{0,2,1:T(8,128)(2,1)}, u32[]{:S(2)}) copy-start(bf16[1024,4,128]{0,2,1:T(8,128)(2,1)} %get-tuple-element.556) | copy-start | bytes 3145732 | tf_op jit(solution)/shard_map/while
  289.9 5.9 %copy-start.24 = (bf16[1024,4,128]{2,0,1:T(8,128)(2,1)S(1)}, bf16[1024,4,128]{2,0,1:T(8,128)(2,1)}, u32[]{:S(2)}) copy-start(bf16[1024,4,128]{2,0,1:T(8,128)(2,1)} %get-tuple-element.557) | copy-start | bytes 3145732 | tf_op jit(solution)/shard_map/while
  300.9 6.2 %copy-start.2 = (f32[4,512,1024]{2,1,0:T(8,128)S(1)}, f32[4,512,1024]{2,1,0:T(8,128)}, u32[]{:S(2)}) copy-start(f32[4,512,1024]{2,1,0:T(8,128)} %copy-done.1) | copy-start | bytes 25165828 | tf_op jit(solution)/shard_map/while
  327.9 30.1 %all-to-all-start.5 = ((bf16[8,2,32768]{2,1,0:T(2,128)(2,1)}), bf16[8,2,32768]{2,1,0:T(2,128)(2,1)}, u32[]{:S(2)}, u32[]{:S(2)}) async-start(bf16[8,2,32768]{2,1,0:T(2,128)(2,1)} %reshape.599), calls=%async_computation.5 | async-start | bytes 2097152 | tf_op jit(solution)/shard_map/all_to_all | solution.py:203
  343.2 19.4 %copy-start.30 = (f32[4096]{0:T(1024)S(1)}, f32[4096]{0:T(1024)}, u32[]{:S(2)}) copy-start(f32[4096]{0:T(1024)} %param.16) | copy-start | bytes 49156
  343.2 19.5 %copy-start.28 = (f32[4096]{0:T(1024)S(1)}, f32[4096]{0:T(1024)}, u32[]{:S(2)}) copy-start(f32[4096]{0:T(1024)} %param.17) | copy-start | bytes 49156
  343.2 19.5 %copy-start.21 = (f32[128,128]{0,1:T(8,128)S(1)}, f32[128,128]{0,1:T(8,128)}, u32[]{:S(2)}) copy-start(f32[128,128]{0,1:T(8,128)} %copy-done.20) | copy-start | bytes 196612
  357.9 45.8 %all-to-all-start.6 = ((bf16[8,2,32768]{2,1,0:T(2,128)(2,1)}), bf16[8,2,32768]{2,1,0:T(2,128)(2,1)}, u32[]{:S(2)}, u32[]{:S(2)}) async-start(bf16[8,2,32768]{2,1,0:T(2,128)(2,1)} %reshape.601), calls=%async_computation.6 | async-start | bytes 2097152 | tf_op jit(solution)/shard_map/all_to_all | solution.py:204
  374.5 10.7 %copy-start.17 = (bf16[2,512,4,128]{3,2,1,0:T(4,128)(2,1)S(1)}, bf16[2,512,4,128]{3,2,1,0:T(4,128)(2,1)}, u32[]{:S(2)}) copy-start(bf16[2,512,4,128]{3,2,1,0:T(4,128)(2,1)} %copy.164) | copy-start | bytes 3145732
  403.7 30.2 %all-to-all-start.7 = ((bf16[8,2,32768]{2,1,0:T(2,128)(2,1)}), bf16[8,2,32768]{2,1,0:T(2,128)(2,1)}, u32[]{:S(2)}, u32[]{:S(2)}) async-start(bf16[8,2,32768]{2,1,0:T(2,128)(2,1)} %reshape.603), calls=%async_computation.7 | async-start | bytes 2097152 | tf_op jit(solution)/shard_map/all_to_all | solution.py:205
  431.5 55.0 %copy-start.4 = (bf16[1,128,4096]{1,2,0:T(8,128)(2,1)S(1)}, bf16[1,128,4096]{1,2,0:T(8,128)(2,1)}, u32[]{:S(2)}) copy-start(bf16[1,128,4096]{1,2,0:T(8,128)(2,1)} %copy-done.3) | copy-start | bytes 3145732
  434.0 78.5 %all-to-all-start.3 = ((bf16[8,2,32768]{2,1,0:T(2,128)(2,1)}), bf16[8,2,32768]{2,1,0:T(2,128)(2,1)}, u32[]{:S(2)}, u32[]{:S(2)}) async-start(bf16[8,2,32768]{2,1,0:T(2,128)(2,1)} %reshape.595), calls=%async_computation.3 | async-start | bytes 2097152 | tf_op jit(solution)/shard_map/all_to_all | solution.py:176
  (30 other events, 77.0 us)
